TPU v7x, 32 devices: a whole 2x2x4 slice. The times are simulated.
32 devices in a mesh: leaf: 8 (over z, x), sub: 4 (over y, core).
Axes of the slice: x: 2, y: 2, z: 4, core: 2. Of those that a mesh axis runs over, the one named last changes fastest.
Arguments:
- points: bfloat16 [96, 64, 512], P('leaf', None, 'sub'), may hold values from -5 to 5
- charges: bfloat16 [96, 8, 512], P('leaf', None, 'sub'), may hold values from -6 to 6
- near_leaf: int32 [96, 32], P('leaf'), may hold values from -1 to 95, as said below
- far_node: int32 [96, 32], P('leaf'), may hold values from 0 to 31
- skel_index: int32 [32, 256], P(('leaf', 'sub')), may hold values from 0 to 1535, as said below
- skel_weight: bfloat16 [32, 8, 256], P(('leaf', 'sub')), may hold values from -12 to 12
Outputs:
- potential: float32 [96, 8, 512], P('leaf', None, 'sub')
Inputs may be any that keep to these rules, and one draw needn't show every extreme that they name: `near_leaf`: entry 0 of the list of leaf l is l itself; every other entry is -1 or a leaf held by another index of leaf. Over the lists of the 12 leaves of one index of leaf no leaf appears twice, and at most 3 distinct leaves of any one other index of leaf appear (leaves k * 12 to k * 12 + 11 belong to index k); every draw reaches 3. `skel_index`: the 256 entries of a row are distinct.
All inputs are finite; a program needn't handle non-finite values.
Results may differ from a plain program's by a relative error of at most 0.0003.
Values may be sent and summed in bfloat16 or wider, within the bound.
A program may use at most 64 MiB of HBM per device.

v0:
```python
import jax
import jax.numpy as jnp
from jax import lax
from jax.sharding import PartitionSpec as P

CAP = 3
RATE_SCALE = 2.5


def kernel_apply(targets, sources, weights):
    target_wide = targets.astype(jnp.float32)
    target_sq = jnp.sum(target_wide * target_wide, axis=0)
    source_sq = jnp.sum(jnp.square(sources.astype(jnp.float32)), axis=1)
    inner_prod = jnp.einsum("dr,mdc->rmc", targets, sources, preferred_element_type=jnp.float32)
    distance = target_sq[:, None, None] + source_sq[None] - 2.0 * inner_prod
    decay_rate = RATE_SCALE / targets.shape[0]
    kernel_block = jnp.exp(-decay_rate * distance)
    return jnp.einsum(
        "rmc,mkc->kr", kernel_block, weights.astype(jnp.float32), precision=lax.Precision.HIGHEST
    )


def shards(points, charges, near_leaf, far_node, skel_index, skel_weight):
    leaf_dev, features, quarter = points.shape
    leaf_count = lax.axis_size("leaf")
    own_index = lax.axis_index("leaf")
    slot_count = CAP
    leaves_all = leaf_count * leaf_dev
    entries = near_leaf.reshape(-1)
    live_flat = entries >= 0
    all_ids = jnp.arange(leaves_all, dtype=jnp.int32)
    lane_ids = jnp.arange(leaf_count, dtype=jnp.int32)
    other_row = lane_ids != own_index
    matches = entries[:, None] == all_ids[None, :]
    wanted = jnp.any(matches, axis=0).reshape(leaf_count, leaf_dev) & other_row[:, None]
    wanted_int = wanted.astype(jnp.int32)
    slot_rank = jnp.cumsum(wanted_int, axis=1) - 1
    asked_mask = lax.all_to_all(wanted_int, "leaf", split_axis=0, concat_axis=0, tiled=True)
    asked_rank = jnp.cumsum(asked_mask, axis=1) - 1
    slot_ids = jnp.arange(slot_count, dtype=jnp.int32)
    selector = (
        (asked_mask[:, None, :] == 1) & (asked_rank[:, None, :] == slot_ids[None, :, None])
    ).astype(jnp.bfloat16)
    send_points = jnp.einsum(
        "dcj,jkq->dckq", selector, points, preferred_element_type=jnp.float32
    ).astype(jnp.bfloat16)
    send_charges = jnp.einsum(
        "dcj,jkq->dckq", selector, charges, preferred_element_type=jnp.float32
    ).astype(jnp.bfloat16)
    got_points, got_charges = (
        lax.all_to_all(send_points, "leaf", split_axis=0, concat_axis=0, tiled=True),
        lax.all_to_all(send_charges, "leaf", split_axis=0, concat_axis=0, tiled=True),
    )
    table_points = jnp.concatenate(
        [points, got_points.reshape(leaf_count * slot_count, features, quarter)], axis=0
    )
    table_charges = jnp.concatenate(
        [charges, got_charges.reshape(leaf_count * slot_count, charges.shape[1], quarter)], axis=0
    )
    slot_pos = leaf_dev + lane_ids[:, None] * slot_count + slot_rank
    local_pos = jnp.broadcast_to(
        jnp.arange(leaf_dev, dtype=jnp.int32)[None, :], (leaf_count, leaf_dev)
    )
    pos_table = jnp.where(other_row[:, None], slot_pos, local_pos).reshape(-1)
    position = jnp.sum(jnp.where(matches, pos_table[None, :], 0), axis=1)
    position = position.reshape(leaf_dev, -1)
    live_mask = live_flat.reshape(leaf_dev, -1)
    whole_targets = lax.all_gather(points, "sub", axis=2, tiled=True)

    def near_targets(pieces):
        target, where_from, alive = pieces
        weights = jnp.where(
            alive[:, None, None], table_charges[where_from], jnp.zeros((), jnp.bfloat16)
        )
        return kernel_apply(target, table_points[where_from], weights)

    partial_value = lax.map(near_targets, (whole_targets, position, live_mask))
    near_term = lax.psum_scatter(partial_value, "sub", scatter_dimension=2, tiled=True)
    node_dev, skel_size = skel_index.shape
    flat_points = jnp.transpose(points, (1, 0, 2)).reshape(features, leaf_dev * quarter)
    picked = jnp.take(flat_points, skel_index.reshape(-1), axis=1)
    skel_points = jnp.transpose(picked.reshape(features, node_dev, skel_size), (1, 0, 2))
    all_skel, all_weight = (
        lax.all_gather(skel_points, ("leaf", "sub"), axis=0, tiled=True),
        lax.all_gather(skel_weight, ("leaf", "sub"), axis=0, tiled=True),
    )

    def far_sum(pieces):
        target, node_list = pieces
        return kernel_apply(target, all_skel[node_list], all_weight[node_list])

    far_term = lax.map(far_sum, (points, far_node))
    return near_term + far_term


def solution(mesh):
    in_specs = (
        P("leaf", None, "sub"),
        P("leaf", None, "sub"),
        P("leaf", None),
        P("leaf", None),
        P(("leaf", "sub"), None),
        P(("leaf", "sub"), None, None),
    )
    out_specs = P("leaf", None, "sub")
    return jax.shard_map(shards, mesh=mesh, in_specs=in_specs, out_specs=out_specs, check_vma=False)
```

profile of v0, /device:TPU:0, one launch (start us, length us, event | category | flops | bytes accessed | tf_op | source)
XLA Modules:
  0.0 407.2 jit_solution(3622828070690735007)
XLA Ops:
  9.1 7.3 %all-to-all-start = ((s32[8,1,12]{2,1,0:T(1,128)}), s32[8,1,12]{2,1,0:T(1,128)S(1)}, u32[]{:S(2)}, u32[]{:S(2)}) async-start(s32[8,1,12]{2,1,0:T(1,128)} %bitcast.13), calls=%async_computation | async-start | bytes 8192 | tf_op jit(solution)/shard_map/all_to_all | solution.py:38
  24.4 4.5 %all-to-all-start.1 = ((bf16[8,3,8,128]{3,2,1,0:T(8,128)(2,1)}), bf16[8,3,8,128]{3,2,1,0:T(8,128)(2,1)S(1)}, u32[]{:S(2)}, u32[]{:S(2)}) async-start(bf16[8,3,8,128]{3,2,1,0:T(8,128)(2,1)} %copy.28), calls=%async_computation.1 | async-start | bytes 98304 | tf_op jit(solution)/shard_map/all_to_all | solution.py:52
  30.9 4.8 %all-to-all-done.1 = bf16[8,3,8,128]{3,2,1,0:T(8,128)(2,1)S(1)} async-done(((bf16[8,3,8,128]{3,2,1,0:T(8,128)(2,1)}), bf16[8,3,8,128]{3,2,1,0:T(8,128)(2,1)S(1)}, u32[]{:S(2)}, u32[]{:S(2)}) %all-to-all-start.1) | async-done | bytes 49184 | tf_op jit(solution)/shard_map/all_to_all | solution.py:52
  35.7 3.5 all-to-all-start.2
  39.2 42.6 %all_gather.10 = bf16[32,8,256]{2,1,0:T(8,128)(2,1)S(1)} all-gather(bf16[1,8,256]{2,1,0:T(8,128)(2,1)} %param.15), channel_id=1, replica_groups=mesh['leaf'=8,'sub'=4] {'leaf','sub'}, dimensions={0}, use_global_device_ids=true | all-gather | bytes 135168 | tf_op jit(solution)/shard_map/all_gather | solution.py:85
  82.5 8.9 %all_gather.9 = bf16[12,64,512]{2,1,0:T(8,128)(2,1)S(1)} all-gather(bf16[12,64,128]{2,1,0:T(8,128)(2,1)} %param.10), channel_id=1, replica_groups=mesh['leaf'=8,'sub'=4] {'sub'}, dimensions={2}, use_global_device_ids=true | all-gather | bytes 983040 | tf_op jit(solution)/shard_map/all_gather | solution.py:68
  91.5 173.4 %while.20 = (s32[]{:T(128)}, f32[12,8,512]{2,1,0:T(8,128)}, pred[12,32]{1,0:T(8,128)(4,1)S(1)}, s32[12,32]{1,0:T(8,128)S(1)}, bf16[36,8,128]{2,1,0:T(8,128)(2,1)...) while((s32[]{:T(128)}, f32[12,8,512]{2,1,0:T(8,128)}, ...), condition=%wide.region_7.8_spmd, body=%wide.region_4.7_spmd.sunk | while | flops 479064672 | bytes 19260740 | solution.py:77
  92.2 4.5 %fusion.87 = f32[512,32,128]{2,0,1:T(8,128)} fusion(bf16[32,64,128]{2,1,0:T(8,128)(2,1)S(1)} %gather_fusion, bf16[12,64,512]{2,1,0:T(8,128)(2,1)S(1)} %get-tuple-element.215, s32[]{:T(128)} %get-tuple-element.202), kind=kOutput, calls=%fused_computation.19.clone.1 | convolution fusion | flops 268435456 | bytes 8978436 | tf_op jit(solution)/shard_map/while/body/eval_jaxpr/dr,mdc->rmc/dot_general | solution.py:14
  97.5 8.5 %fusion.88 = f32[12,8,512]{2,1,0:T(8,128)} fusion(f32[12,8,512]{2,1,0:T(8,128)} %get-tuple-element.203, s32[]{:T(128)} %get-tuple-element.202, f32[512,32,128]{2,0,1:T(8,128)} %fusion.87, f32[32,128]{1,0:T(8,128)S(1)} %multiply_reduce_fusion.8, f32[512]{0:T(512)S(1)} %multiply_reduce_fusion.9, bf16[32,8,128]{2,1,0:T(8,128)(2,1)S(1)} %gather_fusion.1, ...), kind=kOutput, calls=%fused_computation.16.clone.1 | convolution fusion | flops 209747968 | bytes 8489504 | tf_op jit(solution)/shard_map/while/body/eval_jaxpr/rmc,mkc->kr/dot_general | solution.py:18
  106.7 4.5 %fusion.87 = f32[512,32,128]{2,0,1:T(8,128)} fusion(bf16[32,64,128]{2,1,0:T(8,128)(2,1)S(1)} %gather_fusion, bf16[12,64,512]{2,1,0:T(8,128)(2,1)S(1)} %get-tuple-element.215, s32[]{:T(128)} %get-tuple-element.202), kind=kOutput, calls=%fused_computation.19.clone.1 | convolution fusion | flops 268435456 | bytes 8978436 | tf_op jit(solution)/shard_map/while/body/eval_jaxpr/dr,mdc->rmc/dot_general | solution.py:14
  112.0 8.5 %fusion.88 = f32[12,8,512]{2,1,0:T(8,128)} fusion(f32[12,8,512]{2,1,0:T(8,128)} %get-tuple-element.203, s32[]{:T(128)} %get-tuple-element.202, f32[512,32,128]{2,0,1:T(8,128)} %fusion.87, f32[32,128]{1,0:T(8,128)S(1)} %multiply_reduce_fusion.8, f32[512]{0:T(512)S(1)} %multiply_reduce_fusion.9, bf16[32,8,128]{2,1,0:T(8,128)(2,1)S(1)} %gather_fusion.1, ...), kind=kOutput, calls=%fused_computation.16.clone.1 | convolution fusion | flops 209747968 | bytes 8489504 | tf_op jit(solution)/shard_map/while/body/eval_jaxpr/rmc,mkc->kr/dot_general | solution.py:18
  121.1 4.5 %fusion.87 = f32[512,32,128]{2,0,1:T(8,128)} fusion(bf16[32,64,128]{2,1,0:T(8,128)(2,1)S(1)} %gather_fusion, bf16[12,64,512]{2,1,0:T(8,128)(2,1)S(1)} %get-tuple-element.215, s32[]{:T(128)} %get-tuple-element.202), kind=kOutput, calls=%fused_computation.19.clone.1 | convolution fusion | flops 268435456 | bytes 8978436 | tf_op jit(solution)/shard_map/while/body/eval_jaxpr/dr,mdc->rmc/dot_general | solution.py:14
  126.4 8.5 %fusion.88 = f32[12,8,512]{2,1,0:T(8,128)} fusion(f32[12,8,512]{2,1,0:T(8,128)} %get-tuple-element.203, s32[]{:T(128)} %get-tuple-element.202, f32[512,32,128]{2,0,1:T(8,128)} %fusion.87, f32[32,128]{1,0:T(8,128)S(1)} %multiply_reduce_fusion.8, f32[512]{0:T(512)S(1)} %multiply_reduce_fusion.9, bf16[32,8,128]{2,1,0:T(8,128)(2,1)S(1)} %gather_fusion.1, ...), kind=kOutput, calls=%fused_computation.16.clone.1 | convolution fusion | flops 209747968 | bytes 8489504 | tf_op jit(solution)/shard_map/while/body/eval_jaxpr/rmc,mkc->kr/dot_general | solution.py:18
  135.6 4.5 %fusion.87 = f32[512,32,128]{2,0,1:T(8,128)} fusion(bf16[32,64,128]{2,1,0:T(8,128)(2,1)S(1)} %gather_fusion, bf16[12,64,512]{2,1,0:T(8,128)(2,1)S(1)} %get-tuple-element.215, s32[]{:T(128)} %get-tuple-element.202), kind=kOutput, calls=%fused_computation.19.clone.1 | convolution fusion | flops 268435456 | bytes 8978436 | tf_op jit(solution)/shard_map/while/body/eval_jaxpr/dr,mdc->rmc/dot_general | solution.py:14
  140.9 8.5 %fusion.88 = f32[12,8,512]{2,1,0:T(8,128)} fusion(f32[12,8,512]{2,1,0:T(8,128)} %get-tuple-element.203, s32[]{:T(128)} %get-tuple-element.202, f32[512,32,128]{2,0,1:T(8,128)} %fusion.87, f32[32,128]{1,0:T(8,128)S(1)} %multiply_reduce_fusion.8, f32[512]{0:T(512)S(1)} %multiply_reduce_fusion.9, bf16[32,8,128]{2,1,0:T(8,128)(2,1)S(1)} %gather_fusion.1, ...), kind=kOutput, calls=%fused_computation.16.clone.1 | convolution fusion | flops 209747968 | bytes 8489504 | tf_op jit(solution)/shard_map/while/body/eval_jaxpr/rmc,mkc->kr/dot_general | solution.py:18
  150.1 4.5 %fusion.87 = f32[512,32,128]{2,0,1:T(8,128)} fusion(bf16[32,64,128]{2,1,0:T(8,128)(2,1)S(1)} %gather_fusion, bf16[12,64,512]{2,1,0:T(8,128)(2,1)S(1)} %get-tuple-element.215, s32[]{:T(128)} %get-tuple-element.202), kind=kOutput, calls=%fused_computation.19.clone.1 | convolution fusion | flops 268435456 | bytes 8978436 | tf_op jit(solution)/shard_map/while/body/eval_jaxpr/dr,mdc->rmc/dot_general | solution.py:14
  155.3 8.5 %fusion.88 = f32[12,8,512]{2,1,0:T(8,128)} fusion(f32[12,8,512]{2,1,0:T(8,128)} %get-tuple-element.203, s32[]{:T(128)} %get-tuple-element.202, f32[512,32,128]{2,0,1:T(8,128)} %fusion.87, f32[32,128]{1,0:T(8,128)S(1)} %multiply_reduce_fusion.8, f32[512]{0:T(512)S(1)} %multiply_reduce_fusion.9, bf16[32,8,128]{2,1,0:T(8,128)(2,1)S(1)} %gather_fusion.1, ...), kind=kOutput, calls=%fused_computation.16.clone.1 | convolution fusion | flops 209747968 | bytes 8489504 | tf_op jit(solution)/shard_map/while/body/eval_jaxpr/rmc,mkc->kr/dot_general | solution.py:18
  164.5 4.5 %fusion.87 = f32[512,32,128]{2,0,1:T(8,128)} fusion(bf16[32,64,128]{2,1,0:T(8,128)(2,1)S(1)} %gather_fusion, bf16[12,64,512]{2,1,0:T(8,128)(2,1)S(1)} %get-tuple-element.215, s32[]{:T(128)} %get-tuple-element.202), kind=kOutput, calls=%fused_computation.19.clone.1 | convolution fusion | flops 268435456 | bytes 8978436 | tf_op jit(solution)/shard_map/while/body/eval_jaxpr/dr,mdc->rmc/dot_general | solution.py:14
  169.8 8.5 %fusion.88 = f32[12,8,512]{2,1,0:T(8,128)} fusion(f32[12,8,512]{2,1,0:T(8,128)} %get-tuple-element.203, s32[]{:T(128)} %get-tuple-element.202, f32[512,32,128]{2,0,1:T(8,128)} %fusion.87, f32[32,128]{1,0:T(8,128)S(1)} %multiply_reduce_fusion.8, f32[512]{0:T(512)S(1)} %multiply_reduce_fusion.9, bf16[32,8,128]{2,1,0:T(8,128)(2,1)S(1)} %gather_fusion.1, ...), kind=kOutput, calls=%fused_computation.16.clone.1 | convolution fusion | flops 209747968 | bytes 8489504 | tf_op jit(solution)/shard_map/while/body/eval_jaxpr/rmc,mkc->kr/dot_general | solution.py:18
  179.0 4.5 %fusion.87 = f32[512,32,128]{2,0,1:T(8,128)} fusion(bf16[32,64,128]{2,1,0:T(8,128)(2,1)S(1)} %gather_fusion, bf16[12,64,512]{2,1,0:T(8,128)(2,1)S(1)} %get-tuple-element.215, s32[]{:T(128)} %get-tuple-element.202), kind=kOutput, calls=%fused_computation.19.clone.1 | convolution fusion | flops 268435456 | bytes 8978436 | tf_op jit(solution)/shard_map/while/body/eval_jaxpr/dr,mdc->rmc/dot_general | solution.py:14
  184.2 8.5 %fusion.88 = f32[12,8,512]{2,1,0:T(8,128)} fusion(f32[12,8,512]{2,1,0:T(8,128)} %get-tuple-element.203, s32[]{:T(128)} %get-tuple-element.202, f32[512,32,128]{2,0,1:T(8,128)} %fusion.87, f32[32,128]{1,0:T(8,128)S(1)} %multiply_reduce_fusion.8, f32[512]{0:T(512)S(1)} %multiply_reduce_fusion.9, bf16[32,8,128]{2,1,0:T(8,128)(2,1)S(1)} %gather_fusion.1, ...), kind=kOutput, calls=%fused_computation.16.clone.1 | convolution fusion | flops 209747968 | bytes 8489504 | tf_op jit(solution)/shard_map/while/body/eval_jaxpr/rmc,mkc->kr/dot_general | solution.py:18
  193.4 4.5 %fusion.87 = f32[512,32,128]{2,0,1:T(8,128)} fusion(bf16[32,64,128]{2,1,0:T(8,128)(2,1)S(1)} %gather_fusion, bf16[12,64,512]{2,1,0:T(8,128)(2,1)S(1)} %get-tuple-element.215, s32[]{:T(128)} %get-tuple-element.202), kind=kOutput, calls=%fused_computation.19.clone.1 | convolution fusion | flops 268435456 | bytes 8978436 | tf_op jit(solution)/shard_map/while/body/eval_jaxpr/dr,mdc->rmc/dot_general | solution.py:14
  198.7 8.5 %fusion.88 = f32[12,8,512]{2,1,0:T(8,128)} fusion(f32[12,8,512]{2,1,0:T(8,128)} %get-tuple-element.203, s32[]{:T(128)} %get-tuple-element.202, f32[512,32,128]{2,0,1:T(8,128)} %fusion.87, f32[32,128]{1,0:T(8,128)S(1)} %multiply_reduce_fusion.8, f32[512]{0:T(512)S(1)} %multiply_reduce_fusion.9, bf16[32,8,128]{2,1,0:T(8,128)(2,1)S(1)} %gather_fusion.1, ...), kind=kOutput, calls=%fused_computation.16.clone.1 | convolution fusion | flops 209747968 | bytes 8489504 | tf_op jit(solution)/shard_map/while/body/eval_jaxpr/rmc,mkc->kr/dot_general | solution.py:18
  207.9 4.5 %fusion.87 = f32[512,32,128]{2,0,1:T(8,128)} fusion(bf16[32,64,128]{2,1,0:T(8,128)(2,1)S(1)} %gather_fusion, bf16[12,64,512]{2,1,0:T(8,128)(2,1)S(1)} %get-tuple-element.215, s32[]{:T(128)} %get-tuple-element.202), kind=kOutput, calls=%fused_computation.19.clone.1 | convolution fusion | flops 268435456 | bytes 8978436 | tf_op jit(solution)/shard_map/while/body/eval_jaxpr/dr,mdc->rmc/dot_general | solution.py:14
  213.1 8.5 %fusion.88 = f32[12,8,512]{2,1,0:T(8,128)} fusion(f32[12,8,512]{2,1,0:T(8,128)} %get-tuple-element.203, s32[]{:T(128)} %get-tuple-element.202, f32[512,32,128]{2,0,1:T(8,128)} %fusion.87, f32[32,128]{1,0:T(8,128)S(1)} %multiply_reduce_fusion.8, f32[512]{0:T(512)S(1)} %multiply_reduce_fusion.9, bf16[32,8,128]{2,1,0:T(8,128)(2,1)S(1)} %gather_fusion.1, ...), kind=kOutput, calls=%fused_computation.16.clone.1 | convolution fusion | flops 209747968 | bytes 8489504 | tf_op jit(solution)/shard_map/while/body/eval_jaxpr/rmc,mkc->kr/dot_general | solution.py:18
  222.3 4.5 %fusion.87 = f32[512,32,128]{2,0,1:T(8,128)} fusion(bf16[32,64,128]{2,1,0:T(8,128)(2,1)S(1)} %gather_fusion, bf16[12,64,512]{2,1,0:T(8,128)(2,1)S(1)} %get-tuple-element.215, s32[]{:T(128)} %get-tuple-element.202), kind=kOutput, calls=%fused_computation.19.clone.1 | convolution fusion | flops 268435456 | bytes 8978436 | tf_op jit(solution)/shard_map/while/body/eval_jaxpr/dr,mdc->rmc/dot_general | solution.py:14
  227.6 8.5 %fusion.88 = f32[12,8,512]{2,1,0:T(8,128)} fusion(f32[12,8,512]{2,1,0:T(8,128)} %get-tuple-element.203, s32[]{:T(128)} %get-tuple-element.202, f32[512,32,128]{2,0,1:T(8,128)} %fusion.87, f32[32,128]{1,0:T(8,128)S(1)} %multiply_reduce_fusion.8, f32[512]{0:T(512)S(1)} %multiply_reduce_fusion.9, bf16[32,8,128]{2,1,0:T(8,128)(2,1)S(1)} %gather_fusion.1, ...), kind=kOutput, calls=%fused_computation.16.clone.1 | convolution fusion | flops 209747968 | bytes 8489504 | tf_op jit(solution)/shard_map/while/body/eval_jaxpr/rmc,mkc->kr/dot_general | solution.py:18
  236.8 4.5 %fusion.87 = f32[512,32,128]{2,0,1:T(8,128)} fusion(bf16[32,64,128]{2,1,0:T(8,128)(2,1)S(1)} %gather_fusion, bf16[12,64,512]{2,1,0:T(8,128)(2,1)S(1)} %get-tuple-element.215, s32[]{:T(128)} %get-tuple-element.202), kind=kOutput, calls=%fused_computation.19.clone.1 | convolution fusion | flops 268435456 | bytes 8978436 | tf_op jit(solution)/shard_map/while/body/eval_jaxpr/dr,mdc->rmc/dot_general | solution.py:14
  242.0 8.5 %fusion.88 = f32[12,8,512]{2,1,0:T(8,128)} fusion(f32[12,8,512]{2,1,0:T(8,128)} %get-tuple-element.203, s32[]{:T(128)} %get-tuple-element.202, f32[512,32,128]{2,0,1:T(8,128)} %fusion.87, f32[32,128]{1,0:T(8,128)S(1)} %multiply_reduce_fusion.8, f32[512]{0:T(512)S(1)} %multiply_reduce_fusion.9, bf16[32,8,128]{2,1,0:T(8,128)(2,1)S(1)} %gather_fusion.1, ...), kind=kOutput, calls=%fused_computation.16.clone.1 | convolution fusion | flops 209747968 | bytes 8489504 | tf_op jit(solution)/shard_map/while/body/eval_jaxpr/rmc,mkc->kr/dot_general | solution.py:18
  251.2 4.5 %fusion.87 = f32[512,32,128]{2,0,1:T(8,128)} fusion(bf16[32,64,128]{2,1,0:T(8,128)(2,1)S(1)} %gather_fusion, bf16[12,64,512]{2,1,0:T(8,128)(2,1)S(1)} %get-tuple-element.215, s32[]{:T(128)} %get-tuple-element.202), kind=kOutput, calls=%fused_computation.19.clone.1 | convolution fusion | flops 268435456 | bytes 8978436 | tf_op jit(solution)/shard_map/while/body/eval_jaxpr/dr,mdc->rmc/dot_general | solution.py:14
  256.5 8.5 %fusion.88 = f32[12,8,512]{2,1,0:T(8,128)} fusion(f32[12,8,512]{2,1,0:T(8,128)} %get-tuple-element.203, s32[]{:T(128)} %get-tuple-element.202, f32[512,32,128]{2,0,1:T(8,128)} %fusion.87, f32[32,128]{1,0:T(8,128)S(1)} %multiply_reduce_fusion.8, f32[512]{0:T(512)S(1)} %multiply_reduce_fusion.9, bf16[32,8,128]{2,1,0:T(8,128)(2,1)S(1)} %gather_fusion.1, ...), kind=kOutput, calls=%fused_computation.16.clone.1 | convolution fusion | flops 209747968 | bytes 8489504 | tf_op jit(solution)/shard_map/while/body/eval_jaxpr/rmc,mkc->kr/dot_general | solution.py:18
  265.0 133.3 %while.21 = (s32[]{:T(128)}, f32[12,8,128]{2,1,0:T(8,128)S(1)}, s32[12,32]{1,0:T(8,128)}, bf16[32,8,256]{2,1,0:T(8,128)(2,1)S(1)}, bf16[12,64,128]{2,1,0:T(8,128...) while((s32[]{:T(128)}, f32[12,8,128]{2,1,0:T(8,128)S(1)}, s32[12,32]{1,0:T(8,128)}, ...), condition=%wide.region_12.13_spmd, body=%wide.region_9.12_spmd.sunk | while | flops 240665568 | bytes 13084381 | solution.py:92
  271.2 5.0 %fusion.95 = f32[12,8,128]{2,1,0:T(8,128)S(1)} fusion(f32[12,8,128]{2,1,0:T(8,128)S(1)} %get-tuple-element.226, s32[]{:T(128)} %get-tuple-element.225, bf16[32,8,256]{2,1,0:T(8,128)(2,1)S(1)} %gather_fusion.2, f32[128,32,256]{2,0,1:T(8,128)} %fusion.94, f32[32,256]{1,0:T(8,128)S(1)} %multiply_reduce_fusion.10, f32[128]{0:T(128)S(1)} %multiply_reduce_fusion.11), kind=kOutput, calls=%fused_computation.47.clone.1 | convolution fusion | flops 104857600 | bytes 4362756 | tf_op jit(solution)/shard_map/while/body/eval_jaxpr/rmc,mkc->kr/dot_general | solution.py:18
  282.3 5.0 %fusion.95 = f32[12,8,128]{2,1,0:T(8,128)S(1)} fusion(f32[12,8,128]{2,1,0:T(8,128)S(1)} %get-tuple-element.226, s32[]{:T(128)} %get-tuple-element.225, bf16[32,8,256]{2,1,0:T(8,128)(2,1)S(1)} %gather_fusion.2, f32[128,32,256]{2,0,1:T(8,128)} %fusion.94, f32[32,256]{1,0:T(8,128)S(1)} %multiply_reduce_fusion.10, f32[128]{0:T(128)S(1)} %multiply_reduce_fusion.11), kind=kOutput, calls=%fused_computation.47.clone.1 | convolution fusion | flops 104857600 | bytes 4362756 | tf_op jit(solution)/shard_map/while/body/eval_jaxpr/rmc,mkc->kr/dot_general | solution.py:18
  293.4 5.0 %fusion.95 = f32[12,8,128]{2,1,0:T(8,128)S(1)} fusion(f32[12,8,128]{2,1,0:T(8,128)S(1)} %get-tuple-element.226, s32[]{:T(128)} %get-tuple-element.225, bf16[32,8,256]{2,1,0:T(8,128)(2,1)S(1)} %gather_fusion.2, f32[128,32,256]{2,0,1:T(8,128)} %fusion.94, f32[32,256]{1,0:T(8,128)S(1)} %multiply_reduce_fusion.10, f32[128]{0:T(128)S(1)} %multiply_reduce_fusion.11), kind=kOutput, calls=%fused_computation.47.clone.1 | convolution fusion | flops 104857600 | bytes 4362756 | tf_op jit(solution)/shard_map/while/body/eval_jaxpr/rmc,mkc->kr/dot_general | solution.py:18
  300.9 2.7 fusion.94
  304.5 5.0 %fusion.95 = f32[12,8,128]{2,1,0:T(8,128)S(1)} fusion(f32[12,8,128]{2,1,0:T(8,128)S(1)} %get-tuple-element.226, s32[]{:T(128)} %get-tuple-element.225, bf16[32,8,256]{2,1,0:T(8,128)(2,1)S(1)} %gather_fusion.2, f32[128,32,256]{2,0,1:T(8,128)} %fusion.94, f32[32,256]{1,0:T(8,128)S(1)} %multiply_reduce_fusion.10, f32[128]{0:T(128)S(1)} %multiply_reduce_fusion.11), kind=kOutput, calls=%fused_computation.47.clone.1 | convolution fusion | flops 104857600 | bytes 4362756 | tf_op jit(solution)/shard_map/while/body/eval_jaxpr/rmc,mkc->kr/dot_general | solution.py:18
  315.6 5.0 %fusion.95 = f32[12,8,128]{2,1,0:T(8,128)S(1)} fusion(f32[12,8,128]{2,1,0:T(8,128)S(1)} %get-tuple-element.226, s32[]{:T(128)} %get-tuple-element.225, bf16[32,8,256]{2,1,0:T(8,128)(2,1)S(1)} %gather_fusion.2, f32[128,32,256]{2,0,1:T(8,128)} %fusion.94, f32[32,256]{1,0:T(8,128)S(1)} %multiply_reduce_fusion.10, f32[128]{0:T(128)S(1)} %multiply_reduce_fusion.11), kind=kOutput, calls=%fused_computation.47.clone.1 | convolution fusion | flops 104857600 | bytes 4362756 | tf_op jit(solution)/shard_map/while/body/eval_jaxpr/rmc,mkc->kr/dot_general | solution.py:18
  326.7 5.0 %fusion.95 = f32[12,8,128]{2,1,0:T(8,128)S(1)} fusion(f32[12,8,128]{2,1,0:T(8,128)S(1)} %get-tuple-element.226, s32[]{:T(128)} %get-tuple-element.225, bf16[32,8,256]{2,1,0:T(8,128)(2,1)S(1)} %gather_fusion.2, f32[128,32,256]{2,0,1:T(8,128)} %fusion.94, f32[32,256]{1,0:T(8,128)S(1)} %multiply_reduce_fusion.10, f32[128]{0:T(128)S(1)} %multiply_reduce_fusion.11), kind=kOutput, calls=%fused_computation.47.clone.1 | convolution fusion | flops 104857600 | bytes 4362756 | tf_op jit(solution)/shard_map/while/body/eval_jaxpr/rmc,mkc->kr/dot_general | solution.py:18
  334.3 2.7 fusion.94
  337.8 5.0 %fusion.95 = f32[12,8,128]{2,1,0:T(8,128)S(1)} fusion(f32[12,8,128]{2,1,0:T(8,128)S(1)} %get-tuple-element.226, s32[]{:T(128)} %get-tuple-element.225, bf16[32,8,256]{2,1,0:T(8,128)(2,1)S(1)} %gather_fusion.2, f32[128,32,256]{2,0,1:T(8,128)} %fusion.94, f32[32,256]{1,0:T(8,128)S(1)} %multiply_reduce_fusion.10, f32[128]{0:T(128)S(1)} %multiply_reduce_fusion.11), kind=kOutput, calls=%fused_computation.47.clone.1 | convolution fusion | flops 104857600 | bytes 4362756 | tf_op jit(solution)/shard_map/while/body/eval_jaxpr/rmc,mkc->kr/dot_general | solution.py:18
  345.4 2.7 fusion.94
  348.9 5.0 %fusion.95 = f32[12,8,128]{2,1,0:T(8,128)S(1)} fusion(f32[12,8,128]{2,1,0:T(8,128)S(1)} %get-tuple-element.226, s32[]{:T(128)} %get-tuple-element.225, bf16[32,8,256]{2,1,0:T(8,128)(2,1)S(1)} %gather_fusion.2, f32[128,32,256]{2,0,1:T(8,128)} %fusion.94, f32[32,256]{1,0:T(8,128)S(1)} %multiply_reduce_fusion.10, f32[128]{0:T(128)S(1)} %multiply_reduce_fusion.11), kind=kOutput, calls=%fused_computation.47.clone.1 | convolution fusion | flops 104857600 | bytes 4362756 | tf_op jit(solution)/shard_map/while/body/eval_jaxpr/rmc,mkc->kr/dot_general | solution.py:18
  360.0 5.0 %fusion.95 = f32[12,8,128]{2,1,0:T(8,128)S(1)} fusion(f32[12,8,128]{2,1,0:T(8,128)S(1)} %get-tuple-element.226, s32[]{:T(128)} %get-tuple-element.225, bf16[32,8,256]{2,1,0:T(8,128)(2,1)S(1)} %gather_fusion.2, f32[128,32,256]{2,0,1:T(8,128)} %fusion.94, f32[32,256]{1,0:T(8,128)S(1)} %multiply_reduce_fusion.10, f32[128]{0:T(128)S(1)} %multiply_reduce_fusion.11), kind=kOutput, calls=%fused_computation.47.clone.1 | convolution fusion | flops 104857600 | bytes 4362756 | tf_op jit(solution)/shard_map/while/body/eval_jaxpr/rmc,mkc->kr/dot_general | solution.py:18
  367.6 2.7 fusion.94
  371.1 5.0 %fusion.95 = f32[12,8,128]{2,1,0:T(8,128)S(1)} fusion(f32[12,8,128]{2,1,0:T(8,128)S(1)} %get-tuple-element.226, s32[]{:T(128)} %get-tuple-element.225, bf16[32,8,256]{2,1,0:T(8,128)(2,1)S(1)} %gather_fusion.2, f32[128,32,256]{2,0,1:T(8,128)} %fusion.94, f32[32,256]{1,0:T(8,128)S(1)} %multiply_reduce_fusion.10, f32[128]{0:T(128)S(1)} %multiply_reduce_fusion.11), kind=kOutput, calls=%fused_computation.47.clone.1 | convolution fusion | flops 104857600 | bytes 4362756 | tf_op jit(solution)/shard_map/while/body/eval_jaxpr/rmc,mkc->kr/dot_general | solution.py:18
  382.2 5.0 %fusion.95 = f32[12,8,128]{2,1,0:T(8,128)S(1)} fusion(f32[12,8,128]{2,1,0:T(8,128)S(1)} %get-tuple-element.226, s32[]{:T(128)} %get-tuple-element.225, bf16[32,8,256]{2,1,0:T(8,128)(2,1)S(1)} %gather_fusion.2, f32[128,32,256]{2,0,1:T(8,128)} %fusion.94, f32[32,256]{1,0:T(8,128)S(1)} %multiply_reduce_fusion.10, f32[128]{0:T(128)S(1)} %multiply_reduce_fusion.11), kind=kOutput, calls=%fused_computation.47.clone.1 | convolution fusion | flops 104857600 | bytes 4362756 | tf_op jit(solution)/shard_map/while/body/eval_jaxpr/rmc,mkc->kr/dot_general | solution.py:18
  393.3 5.0 %fusion.95 = f32[12,8,128]{2,1,0:T(8,128)S(1)} fusion(f32[12,8,128]{2,1,0:T(8,128)S(1)} %get-tuple-element.226, s32[]{:T(128)} %get-tuple-element.225, bf16[32,8,256]{2,1,0:T(8,128)(2,1)S(1)} %gather_fusion.2, f32[128,32,256]{2,0,1:T(8,128)} %fusion.94, f32[32,256]{1,0:T(8,128)S(1)} %multiply_reduce_fusion.10, f32[128]{0:T(128)S(1)} %multiply_reduce_fusion.11), kind=kOutput, calls=%fused_computation.47.clone.1 | convolution fusion | flops 104857600 | bytes 4362756 | tf_op jit(solution)/shard_map/while/body/eval_jaxpr/rmc,mkc->kr/dot_general | solution.py:18
  (209 shorter events, 93.6 us)
Async XLA Ops:
  7.4 84.1 %copy-start = (bf16[12,64,128]{2,1,0:T(8,128)(2,1)S(1)}, bf16[12,64,128]{2,1,0:T(8,128)(2,1)}, u32[]{:S(2)}) copy-start(bf16[12,64,128]{2,1,0:T(8,128)(2,1)} %param.10) | copy-start | bytes 589828
  7.4 84.1 %copy-start.1 = (bf16[12,8,128]{2,1,0:T(8,128)(2,1)S(1)}, bf16[12,8,128]{2,1,0:T(8,128)(2,1)}, u32[]{:S(2)}) copy-start(bf16[12,8,128]{2,1,0:T(8,128)(2,1)} %param.11) | copy-start | bytes 73732
  9.1 13.6 %all-to-all-start = ((s32[8,1,12]{2,1,0:T(1,128)}), s32[8,1,12]{2,1,0:T(1,128)S(1)}, u32[]{:S(2)}, u32[]{:S(2)}) async-start(s32[8,1,12]{2,1,0:T(1,128)} %bitcast.13), calls=%async_computation | async-start | bytes 8192 | tf_op jit(solution)/shard_map/all_to_all | solution.py:38
  16.3 248.7 %all-gather.2.cloned.1.call-start = ((), (), s32[]{:S(2)}) async-start(), calls=%async_computation.5 | async-start | bytes 1081344 | tf_op jit(solution)/shard_map/all_gather | solution.py:84
  24.4 11.3 %all-to-all-start.1 = ((bf16[8,3,8,128]{3,2,1,0:T(8,128)(2,1)}), bf16[8,3,8,128]{3,2,1,0:T(8,128)(2,1)S(1)}, u32[]{:S(2)}, u32[]{:S(2)}) async-start(bf16[8,3,8,128]{3,2,1,0:T(8,128)(2,1)} %copy.28), calls=%async_computation.1 | async-start | bytes 98304 | tf_op jit(solution)/shard_map/all_to_all | solution.py:52
  35.7 55.7 %all-to-all-start.2 = ((bf16[8,3,64,128]{3,2,1,0:T(8,128)(2,1)}), bf16[8,3,64,128]{3,2,1,0:T(8,128)(2,1)S(1)}, u32[]{:S(2)}, u32[]{:S(2)}) async-start(bf16[8,3,64,128]{3,2,1,0:T(8,128)(2,1)} %copy.30), calls=%async_computation.2 | async-start | bytes 786432 | tf_op jit(solution)/shard_map/all_to_all | solution.py:51
  39.2 359.1 %reduce-scatter.2.cloned.1.call-start = ((), (), s32[]{:S(2)}) async-start(), calls=%async_computation.4 | async-start | bytes 245760 | tf_op jit(solution)/shard_map/reduce_scatter | solution.py:78
Sparse Core Ops, SparseCore 0:
  20.7 56.8 all-gather.1
Sparse Core Ops, SparseCore 1:
  265.1 15.8 reduce-scatter.1
where the time goes:
time: 409 us; the launch traced here: 407 us
  matrix products  250 us (61%)
  blocking collectives  51.5 us (13%)
  local copies, waits for them, and re-layouts  49.3 us (12%)
  other arithmetic  19.5 us (5%)
  starting transfers between devices  15.3 us (4%)
  between operations  15 us (4%)
  waiting for transfers between devices  6.28 us (2%)
    dot_general x24, matrix products, kernel_apply(): jnp.einsum('rmc,mkc->kr', kernel_block, weights.astype(jnp.float32), prec...  162 us
    dot_general x24, matrix products, kernel_apply(): jnp.einsum('dr,mdc->rmc', targets, sources, preferred_element_type=jnp.fl...  86 us
    all_gather x1, blocking collectives, shards(): lax.all_gather(skel_weight, ('leaf', 'sub'), axis=0, tiled=True)  42.6 us
    gather x24, local copies, waits for them, and re-layouts, far_sum(): return kernel_apply(target, all_skel[node_list], all_weight[node_list])  28.9 us
    all_gather x1, blocking collectives, shards(): whole_targets = lax.all_gather(points, 'sub', axis=2, tiled=True)  8.93 us
    select_n x12, other arithmetic, far_sum(): return kernel_apply(target, all_skel[node_list], all_weight[node_list])  8.59 us
  transfers between devices with their start and end apart: 5, of which 2 were waited for; matrix products, arithmetic and copies ran while one was open for 77% of the time, Pallas kernels for 0%

commit v1 on v0

--- a/solution.py
+++ b/solution.py
@@ -5,6 +5,28 @@
 
 CAP = 3
 RATE_SCALE = 2.5
+
+
+def in_order(pieces, dim):
+    pieces = jnp.moveaxis(pieces, 0, dim)
+    shape = pieces.shape
+    return pieces.reshape(*shape[:dim], shape[dim] * shape[dim + 1], *shape[dim + 2 :])
+
+
+def doubled(x, axis):
+    size = lax.axis_size(axis)
+    tiles = x[None]
+    for level in range(size.bit_length() - 1):
+        bit = 1 << level
+        received = lax.ppermute(tiles, axis, [(i, i ^ bit) for i in range(size)])
+        both = jnp.stack([tiles, received])
+        upper = lax.axis_index(axis) >> level & 1
+        tiles = jnp.where(upper == 0, both, both[::-1]).reshape(-1, *x.shape)
+    return tiles
+
+
+def doubled_up(x, axis, dim):
+    return in_order(doubled(x, axis), dim)
 
 
 def kernel_apply(targets, sources, weights):
@@ -82,7 +104,7 @@
     skel_points = jnp.transpose(picked.reshape(features, node_dev, skel_size), (1, 0, 2))
     all_skel, all_weight = (
         lax.all_gather(skel_points, ("leaf", "sub"), axis=0, tiled=True),
-        lax.all_gather(skel_weight, ("leaf", "sub"), axis=0, tiled=True),
+        doubled_up(skel_weight, ("leaf", "sub"), 0),
     )
 
     def far_sum(pieces):

time: 409 us -> 335 us (0.82)
  matrix products: 250 us -> 201 us
  blocking collectives: 51.5 us -> 9.06 us
  starting transfers between devices: 15.3 us -> 23.8 us
  waiting for transfers between devices: 6.28 us -> 14.7 us
    all_gather x1 -> x0, blocking collectives: 42.6 us -> none  [shards(): lax.all_gather(skel_weight, ('leaf', 'sub'), axis=0, tiled=True)]
    dot_general x24, matrix products: 162 us -> 136 us  [kernel_apply(): jnp.einsum('rmc,mkc->kr', kernel_block, weights.astype(jnp.float32), prec...]
    dot_general x24, matrix products: 86 us -> 62.8 us  [kernel_apply(): jnp.einsum('dr,mdc->rmc', targets, sources, preferred_element_type=jnp.fl...]
    ppermute x0 -> x5, waiting for transfers between devices: none -> 12 us  [doubled(): received = lax.ppermute(tiles, axis, [(i, i ^ bit) for i in range(size)])]
    ppermute x0 -> x5, starting transfers between devices: none -> 8.5 us  [doubled(): received = lax.ppermute(tiles, axis, [(i, i ^ bit) for i in range(size)])]
  transfers between devices with their start and end apart: 5 -> 10, of which waited for: 2 -> 3; matrix products, arithmetic and copies ran while one was open for 77% -> 80% of each run, Pallas kernels for 0% -> 0%
where the time goes in v1:
time: 335 us; the launch traced here: 333 us
  matrix products  201 us (60%)
  local copies, waits for them, and re-layouts  49.2 us (15%)
  starting transfers between devices  23.8 us (7%)
  other arithmetic  20.3 us (6%)
  between operations  15 us (4%)
  waiting for transfers between devices  14.7 us (4%)
  blocking collectives  9.06 us (3%)
    dot_general x24, matrix products, kernel_apply(): jnp.einsum('rmc,mkc->kr', kernel_block, weights.astype(jnp.float32), prec...  136 us
    dot_general x24, matrix products, kernel_apply(): jnp.einsum('dr,mdc->rmc', targets, sources, preferred_element_type=jnp.fl...  62.8 us
    gather x24, local copies, waits for them, and re-layouts, far_sum(): return kernel_apply(target, all_skel[node_list], all_weight[node_list])  28.9 us
    ppermute x5, waiting for transfers between devices, doubled(): received = lax.ppermute(tiles, axis, [(i, i ^ bit) for i in range(size)])  12 us
    all_gather x1, blocking collectives, shards(): whole_targets = lax.all_gather(points, 'sub', axis=2, tiled=True)  9.06 us
    select_n x12, other arithmetic, far_sum(): return kernel_apply(target, all_skel[node_list], all_weight[node_list])  8.58 us
    ppermute x5, starting transfers between devices, doubled(): received = lax.ppermute(tiles, axis, [(i, i ^ bit) for i in range(size)])  8.5 us
    gather x12, local copies, waits for them, and re-layouts, near_targets(): return kernel_apply(target, table_points[where_from], weights)  7.76 us
  transfers between devices with their start and end apart: 10, of which 3 were waited for; matrix products, arithmetic and copies ran while one was open for 80% of the time, Pallas kernels for 0%

profile of v1, /device:TPU:0, one launch (start us, length us, event | category | flops | bytes accessed | tf_op | source)
XLA Modules:
  0.0 333.3 jit_solution(15807581544696674657)
XLA Ops:
  9.1 7.3 %all-to-all-start = ((s32[8,1,12]{2,1,0:T(1,128)}), s32[8,1,12]{2,1,0:T(1,128)S(1)}, u32[]{:S(2)}, u32[]{:S(2)}) async-start(s32[8,1,12]{2,1,0:T(1,128)} %bitcast.13), calls=%async_computation | async-start | bytes 8192 | tf_op jit(solution)/shard_map/all_to_all | solution.py:60
  21.5 9.1 %all_gather.6 = bf16[12,64,512]{2,1,0:T(8,128)(2,1)S(1)} all-gather(bf16[12,64,128]{2,1,0:T(8,128)(2,1)} %param.10), channel_id=1, replica_groups=mesh['leaf'=8,'sub'=4] {'sub'}, dimensions={2}, use_global_device_ids=true | all-gather | bytes 983040 | tf_op jit(solution)/shard_map/all_gather | solution.py:90
  33.5 2.1 collective-permute-done.1
  35.7 2.0 collective-permute-start.2
  39.2 4.5 %all-to-all-start.1 = ((bf16[8,3,8,128]{3,2,1,0:T(8,128)(2,1)}), bf16[8,3,8,128]{3,2,1,0:T(8,128)(2,1)S(1)}, u32[]{:S(2)}, u32[]{:S(2)}) async-start(bf16[8,3,8,128]{3,2,1,0:T(8,128)(2,1)} %copy.31), calls=%async_computation.1 | async-start | bytes 98304 | tf_op jit(solution)/shard_map/all_to_all | solution.py:74
  43.7 2.1 collective-permute-start.3
  47.8 2.7 all-to-all-done.1
  50.5 3.5 %all-to-all-start.2 = ((bf16[8,3,64,128]{3,2,1,0:T(8,128)(2,1)}), bf16[8,3,64,128]{3,2,1,0:T(8,128)(2,1)S(1)}, u32[]{:S(2)}, u32[]{:S(2)}) async-start(bf16[8,3,64,128]{3,2,1,0:T(8,128)(2,1)} %copy.33), calls=%async_computation.2 | async-start | bytes 786432 | tf_op jit(solution)/shard_map/all_to_all | solution.py:73
  54.1 2.9 collective-permute-start.4
  56.9 9.8 %collective-permute-done.4 = bf16[16,1,8,256]{3,2,0,1:T(8,128)(2,1)S(1)} collective-permute-done((bf16[16,1,8,256]{3,2,0,1:T(8,128)(2,1)S(1)}, bf16[16,1,8,256]{3,2,0,1:T(8,128)(2,1)S(1)}, u32[]{:S(2)}, u32[]{:S(2)}) %collective-permute-start.4) | collective-permute-done | bytes 65568 | tf_op jit(solution)/shard_map/ppermute | solution.py:21
  66.9 173.5 %while.20 = (s32[]{:T(128)}, f32[12,8,512]{2,1,0:T(8,128)}, pred[12,32]{1,0:T(8,128)(4,1)S(1)}, s32[12,32]{1,0:T(8,128)S(1)}, bf16[36,8,128]{2,1,0:T(8,128)(2,1)...) while((s32[]{:T(128)}, f32[12,8,512]{2,1,0:T(8,128)}, ...), condition=%wide.region_7.8_spmd, body=%wide.region_4.7_spmd.sunk | while | flops 479064672 | bytes 19260240 | solution.py:99
  67.6 4.5 %fusion.89 = f32[512,32,128]{2,0,1:T(8,128)} fusion(bf16[32,64,128]{2,1,0:T(8,128)(2,1)S(1)} %gather_fusion, bf16[12,64,512]{2,1,0:T(8,128)(2,1)S(1)} %get-tuple-element.217, s32[]{:T(128)S(6)} %copy.50), kind=kOutput, calls=%fused_computation.19.clone.1 | convolution fusion | flops 268435456 | bytes 8978436 | tf_op jit(solution)/shard_map/while/body/eval_jaxpr/dr,mdc->rmc/dot_general | solution.py:36
  72.9 8.5 %fusion.90 = f32[12,8,512]{2,1,0:T(8,128)} fusion(f32[12,8,512]{2,1,0:T(8,128)} %get-tuple-element.205, s32[]{:T(128)S(6)} %copy.50, f32[512,32,128]{2,0,1:T(8,128)} %fusion.89, f32[32,128]{1,0:T(8,128)S(1)} %multiply_reduce_fusion.8, f32[512]{0:T(512)S(1)} %multiply_reduce_fusion.9, bf16[32,8,128]{2,1,0:T(8,128)(2,1)S(1)} %gather_fusion.1, ...), kind=kOutput, calls=%fused_computation.16.clone.1 | convolution fusion | flops 209747968 | bytes 8488996 | tf_op jit(solution)/shard_map/while/body/eval_jaxpr/rmc,mkc->kr/dot_general | solution.py:40
  82.1 4.5 %fusion.89 = f32[512,32,128]{2,0,1:T(8,128)} fusion(bf16[32,64,128]{2,1,0:T(8,128)(2,1)S(1)} %gather_fusion, bf16[12,64,512]{2,1,0:T(8,128)(2,1)S(1)} %get-tuple-element.217, s32[]{:T(128)S(6)} %copy.50), kind=kOutput, calls=%fused_computation.19.clone.1 | convolution fusion | flops 268435456 | bytes 8978436 | tf_op jit(solution)/shard_map/while/body/eval_jaxpr/dr,mdc->rmc/dot_general | solution.py:36
  87.4 8.5 %fusion.90 = f32[12,8,512]{2,1,0:T(8,128)} fusion(f32[12,8,512]{2,1,0:T(8,128)} %get-tuple-element.205, s32[]{:T(128)S(6)} %copy.50, f32[512,32,128]{2,0,1:T(8,128)} %fusion.89, f32[32,128]{1,0:T(8,128)S(1)} %multiply_reduce_fusion.8, f32[512]{0:T(512)S(1)} %multiply_reduce_fusion.9, bf16[32,8,128]{2,1,0:T(8,128)(2,1)S(1)} %gather_fusion.1, ...), kind=kOutput, calls=%fused_computation.16.clone.1 | convolution fusion | flops 209747968 | bytes 8488996 | tf_op jit(solution)/shard_map/while/body/eval_jaxpr/rmc,mkc->kr/dot_general | solution.py:40
  96.5 4.5 %fusion.89 = f32[512,32,128]{2,0,1:T(8,128)} fusion(bf16[32,64,128]{2,1,0:T(8,128)(2,1)S(1)} %gather_fusion, bf16[12,64,512]{2,1,0:T(8,128)(2,1)S(1)} %get-tuple-element.217, s32[]{:T(128)S(6)} %copy.50), kind=kOutput, calls=%fused_computation.19.clone.1 | convolution fusion | flops 268435456 | bytes 8978436 | tf_op jit(solution)/shard_map/while/body/eval_jaxpr/dr,mdc->rmc/dot_general | solution.py:36
  101.8 8.5 %fusion.90 = f32[12,8,512]{2,1,0:T(8,128)} fusion(f32[12,8,512]{2,1,0:T(8,128)} %get-tuple-element.205, s32[]{:T(128)S(6)} %copy.50, f32[512,32,128]{2,0,1:T(8,128)} %fusion.89, f32[32,128]{1,0:T(8,128)S(1)} %multiply_reduce_fusion.8, f32[512]{0:T(512)S(1)} %multiply_reduce_fusion.9, bf16[32,8,128]{2,1,0:T(8,128)(2,1)S(1)} %gather_fusion.1, ...), kind=kOutput, calls=%fused_computation.16.clone.1 | convolution fusion | flops 209747968 | bytes 8488996 | tf_op jit(solution)/shard_map/while/body/eval_jaxpr/rmc,mkc->kr/dot_general | solution.py:40
  111.0 4.5 %fusion.89 = f32[512,32,128]{2,0,1:T(8,128)} fusion(bf16[32,64,128]{2,1,0:T(8,128)(2,1)S(1)} %gather_fusion, bf16[12,64,512]{2,1,0:T(8,128)(2,1)S(1)} %get-tuple-element.217, s32[]{:T(128)S(6)} %copy.50), kind=kOutput, calls=%fused_computation.19.clone.1 | convolution fusion | flops 268435456 | bytes 8978436 | tf_op jit(solution)/shard_map/while/body/eval_jaxpr/dr,mdc->rmc/dot_general | solution.py:36
  116.3 8.5 %fusion.90 = f32[12,8,512]{2,1,0:T(8,128)} fusion(f32[12,8,512]{2,1,0:T(8,128)} %get-tuple-element.205, s32[]{:T(128)S(6)} %copy.50, f32[512,32,128]{2,0,1:T(8,128)} %fusion.89, f32[32,128]{1,0:T(8,128)S(1)} %multiply_reduce_fusion.8, f32[512]{0:T(512)S(1)} %multiply_reduce_fusion.9, bf16[32,8,128]{2,1,0:T(8,128)(2,1)S(1)} %gather_fusion.1, ...), kind=kOutput, calls=%fused_computation.16.clone.1 | convolution fusion | flops 209747968 | bytes 8488996 | tf_op jit(solution)/shard_map/while/body/eval_jaxpr/rmc,mkc->kr/dot_general | solution.py:40
  125.4 4.5 %fusion.89 = f32[512,32,128]{2,0,1:T(8,128)} fusion(bf16[32,64,128]{2,1,0:T(8,128)(2,1)S(1)} %gather_fusion, bf16[12,64,512]{2,1,0:T(8,128)(2,1)S(1)} %get-tuple-element.217, s32[]{:T(128)S(6)} %copy.50), kind=kOutput, calls=%fused_computation.19.clone.1 | convolution fusion | flops 268435456 | bytes 8978436 | tf_op jit(solution)/shard_map/while/body/eval_jaxpr/dr,mdc->rmc/dot_general | solution.py:36
  130.7 8.5 %fusion.90 = f32[12,8,512]{2,1,0:T(8,128)} fusion(f32[12,8,512]{2,1,0:T(8,128)} %get-tuple-element.205, s32[]{:T(128)S(6)} %copy.50, f32[512,32,128]{2,0,1:T(8,128)} %fusion.89, f32[32,128]{1,0:T(8,128)S(1)} %multiply_reduce_fusion.8, f32[512]{0:T(512)S(1)} %multiply_reduce_fusion.9, bf16[32,8,128]{2,1,0:T(8,128)(2,1)S(1)} %gather_fusion.1, ...), kind=kOutput, calls=%fused_computation.16.clone.1 | convolution fusion | flops 209747968 | bytes 8488996 | tf_op jit(solution)/shard_map/while/body/eval_jaxpr/rmc,mkc->kr/dot_general | solution.py:40
  139.9 4.5 %fusion.89 = f32[512,32,128]{2,0,1:T(8,128)} fusion(bf16[32,64,128]{2,1,0:T(8,128)(2,1)S(1)} %gather_fusion, bf16[12,64,512]{2,1,0:T(8,128)(2,1)S(1)} %get-tuple-element.217, s32[]{:T(128)S(6)} %copy.50), kind=kOutput, calls=%fused_computation.19.clone.1 | convolution fusion | flops 268435456 | bytes 8978436 | tf_op jit(solution)/shard_map/while/body/eval_jaxpr/dr,mdc->rmc/dot_general | solution.py:36
  145.2 8.5 %fusion.90 = f32[12,8,512]{2,1,0:T(8,128)} fusion(f32[12,8,512]{2,1,0:T(8,128)} %get-tuple-element.205, s32[]{:T(128)S(6)} %copy.50, f32[512,32,128]{2,0,1:T(8,128)} %fusion.89, f32[32,128]{1,0:T(8,128)S(1)} %multiply_reduce_fusion.8, f32[512]{0:T(512)S(1)} %multiply_reduce_fusion.9, bf16[32,8,128]{2,1,0:T(8,128)(2,1)S(1)} %gather_fusion.1, ...), kind=kOutput, calls=%fused_computation.16.clone.1 | convolution fusion | flops 209747968 | bytes 8488996 | tf_op jit(solution)/shard_map/while/body/eval_jaxpr/rmc,mkc->kr/dot_general | solution.py:40
  154.3 4.5 %fusion.89 = f32[512,32,128]{2,0,1:T(8,128)} fusion(bf16[32,64,128]{2,1,0:T(8,128)(2,1)S(1)} %gather_fusion, bf16[12,64,512]{2,1,0:T(8,128)(2,1)S(1)} %get-tuple-element.217, s32[]{:T(128)S(6)} %copy.50), kind=kOutput, calls=%fused_computation.19.clone.1 | convolution fusion | flops 268435456 | bytes 8978436 | tf_op jit(solution)/shard_map/while/body/eval_jaxpr/dr,mdc->rmc/dot_general | solution.py:36
  159.6 8.5 %fusion.90 = f32[12,8,512]{2,1,0:T(8,128)} fusion(f32[12,8,512]{2,1,0:T(8,128)} %get-tuple-element.205, s32[]{:T(128)S(6)} %copy.50, f32[512,32,128]{2,0,1:T(8,128)} %fusion.89, f32[32,128]{1,0:T(8,128)S(1)} %multiply_reduce_fusion.8, f32[512]{0:T(512)S(1)} %multiply_reduce_fusion.9, bf16[32,8,128]{2,1,0:T(8,128)(2,1)S(1)} %gather_fusion.1, ...), kind=kOutput, calls=%fused_computation.16.clone.1 | convolution fusion | flops 209747968 | bytes 8488996 | tf_op jit(solution)/shard_map/while/body/eval_jaxpr/rmc,mkc->kr/dot_general | solution.py:40
  168.8 4.5 %fusion.89 = f32[512,32,128]{2,0,1:T(8,128)} fusion(bf16[32,64,128]{2,1,0:T(8,128)(2,1)S(1)} %gather_fusion, bf16[12,64,512]{2,1,0:T(8,128)(2,1)S(1)} %get-tuple-element.217, s32[]{:T(128)S(6)} %copy.50), kind=kOutput, calls=%fused_computation.19.clone.1 | convolution fusion | flops 268435456 | bytes 8978436 | tf_op jit(solution)/shard_map/while/body/eval_jaxpr/dr,mdc->rmc/dot_general | solution.py:36
  174.1 8.5 %fusion.90 = f32[12,8,512]{2,1,0:T(8,128)} fusion(f32[12,8,512]{2,1,0:T(8,128)} %get-tuple-element.205, s32[]{:T(128)S(6)} %copy.50, f32[512,32,128]{2,0,1:T(8,128)} %fusion.89, f32[32,128]{1,0:T(8,128)S(1)} %multiply_reduce_fusion.8, f32[512]{0:T(512)S(1)} %multiply_reduce_fusion.9, bf16[32,8,128]{2,1,0:T(8,128)(2,1)S(1)} %gather_fusion.1, ...), kind=kOutput, calls=%fused_computation.16.clone.1 | convolution fusion | flops 209747968 | bytes 8488996 | tf_op jit(solution)/shard_map/while/body/eval_jaxpr/rmc,mkc->kr/dot_general | solution.py:40
  183.2 4.5 %fusion.89 = f32[512,32,128]{2,0,1:T(8,128)} fusion(bf16[32,64,128]{2,1,0:T(8,128)(2,1)S(1)} %gather_fusion, bf16[12,64,512]{2,1,0:T(8,128)(2,1)S(1)} %get-tuple-element.217, s32[]{:T(128)S(6)} %copy.50), kind=kOutput, calls=%fused_computation.19.clone.1 | convolution fusion | flops 268435456 | bytes 8978436 | tf_op jit(solution)/shard_map/while/body/eval_jaxpr/dr,mdc->rmc/dot_general | solution.py:36
  188.5 8.5 %fusion.90 = f32[12,8,512]{2,1,0:T(8,128)} fusion(f32[12,8,512]{2,1,0:T(8,128)} %get-tuple-element.205, s32[]{:T(128)S(6)} %copy.50, f32[512,32,128]{2,0,1:T(8,128)} %fusion.89, f32[32,128]{1,0:T(8,128)S(1)} %multiply_reduce_fusion.8, f32[512]{0:T(512)S(1)} %multiply_reduce_fusion.9, bf16[32,8,128]{2,1,0:T(8,128)(2,1)S(1)} %gather_fusion.1, ...), kind=kOutput, calls=%fused_computation.16.clone.1 | convolution fusion | flops 209747968 | bytes 8488996 | tf_op jit(solution)/shard_map/while/body/eval_jaxpr/rmc,mkc->kr/dot_general | solution.py:40
  197.7 4.5 %fusion.89 = f32[512,32,128]{2,0,1:T(8,128)} fusion(bf16[32,64,128]{2,1,0:T(8,128)(2,1)S(1)} %gather_fusion, bf16[12,64,512]{2,1,0:T(8,128)(2,1)S(1)} %get-tuple-element.217, s32[]{:T(128)S(6)} %copy.50), kind=kOutput, calls=%fused_computation.19.clone.1 | convolution fusion | flops 268435456 | bytes 8978436 | tf_op jit(solution)/shard_map/while/body/eval_jaxpr/dr,mdc->rmc/dot_general | solution.py:36
  203.0 8.5 %fusion.90 = f32[12,8,512]{2,1,0:T(8,128)} fusion(f32[12,8,512]{2,1,0:T(8,128)} %get-tuple-element.205, s32[]{:T(128)S(6)} %copy.50, f32[512,32,128]{2,0,1:T(8,128)} %fusion.89, f32[32,128]{1,0:T(8,128)S(1)} %multiply_reduce_fusion.8, f32[512]{0:T(512)S(1)} %multiply_reduce_fusion.9, bf16[32,8,128]{2,1,0:T(8,128)(2,1)S(1)} %gather_fusion.1, ...), kind=kOutput, calls=%fused_computation.16.clone.1 | convolution fusion | flops 209747968 | bytes 8488996 | tf_op jit(solution)/shard_map/while/body/eval_jaxpr/rmc,mkc->kr/dot_general | solution.py:40
  212.1 4.5 %fusion.89 = f32[512,32,128]{2,0,1:T(8,128)} fusion(bf16[32,64,128]{2,1,0:T(8,128)(2,1)S(1)} %gather_fusion, bf16[12,64,512]{2,1,0:T(8,128)(2,1)S(1)} %get-tuple-element.217, s32[]{:T(128)S(6)} %copy.50), kind=kOutput, calls=%fused_computation.19.clone.1 | convolution fusion | flops 268435456 | bytes 8978436 | tf_op jit(solution)/shard_map/while/body/eval_jaxpr/dr,mdc->rmc/dot_general | solution.py:36
  217.4 8.5 %fusion.90 = f32[12,8,512]{2,1,0:T(8,128)} fusion(f32[12,8,512]{2,1,0:T(8,128)} %get-tuple-element.205, s32[]{:T(128)S(6)} %copy.50, f32[512,32,128]{2,0,1:T(8,128)} %fusion.89, f32[32,128]{1,0:T(8,128)S(1)} %multiply_reduce_fusion.8, f32[512]{0:T(512)S(1)} %multiply_reduce_fusion.9, bf16[32,8,128]{2,1,0:T(8,128)(2,1)S(1)} %gather_fusion.1, ...), kind=kOutput, calls=%fused_computation.16.clone.1 | convolution fusion | flops 209747968 | bytes 8488996 | tf_op jit(solution)/shard_map/while/body/eval_jaxpr/rmc,mkc->kr/dot_general | solution.py:40
  226.6 4.5 %fusion.89 = f32[512,32,128]{2,0,1:T(8,128)} fusion(bf16[32,64,128]{2,1,0:T(8,128)(2,1)S(1)} %gather_fusion, bf16[12,64,512]{2,1,0:T(8,128)(2,1)S(1)} %get-tuple-element.217, s32[]{:T(128)S(6)} %copy.50), kind=kOutput, calls=%fused_computation.19.clone.1 | convolution fusion | flops 268435456 | bytes 8978436 | tf_op jit(solution)/shard_map/while/body/eval_jaxpr/dr,mdc->rmc/dot_general | solution.py:36
  231.9 8.5 %fusion.90 = f32[12,8,512]{2,1,0:T(8,128)} fusion(f32[12,8,512]{2,1,0:T(8,128)} %get-tuple-element.205, s32[]{:T(128)S(6)} %copy.50, f32[512,32,128]{2,0,1:T(8,128)} %fusion.89, f32[32,128]{1,0:T(8,128)S(1)} %multiply_reduce_fusion.8, f32[512]{0:T(512)S(1)} %multiply_reduce_fusion.9, bf16[32,8,128]{2,1,0:T(8,128)(2,1)S(1)} %gather_fusion.1, ...), kind=kOutput, calls=%fused_computation.16.clone.1 | convolution fusion | flops 209747968 | bytes 8488996 | tf_op jit(solution)/shard_map/while/body/eval_jaxpr/rmc,mkc->kr/dot_general | solution.py:40
  240.4 84.0 %while.21 = (s32[]{:T(128)}, f32[12,8,128]{2,1,0:T(8,128)S(1)}, s32[12,32]{1,0:T(8,128)}, bf16[32,8,256]{2,1,0:T(8,128)(2,1)S(1)}, bf16[12,64,128]{2,1,0:T(8,128...) while((s32[]{:T(128)}, f32[12,8,128]{2,1,0:T(8,128)S(1)}, s32[12,32]{1,0:T(8,128)}, ...), condition=%wide.region_12.13_spmd, body=%wide.region_9.12_spmd.sunk | while | flops 240665568 | bytes 13084389 | solution.py:114
  244.6 2.8 fusion.97
  251.6 2.8 fusion.97
  258.6 2.8 fusion.97
  265.6 2.8 fusion.97
  272.6 2.8 fusion.97
  279.6 2.8 fusion.97
  286.6 2.8 fusion.97
  293.6 2.8 fusion.97
  300.6 2.8 fusion.97
  307.6 2.8 fusion.97
  314.6 2.8 fusion.97
  321.6 2.8 fusion.97
  (228 shorter events, 82.1 us)
Async XLA Ops:
  7.4 59.5 %copy-start = (bf16[12,64,128]{2,1,0:T(8,128)(2,1)S(1)}, bf16[12,64,128]{2,1,0:T(8,128)(2,1)}, u32[]{:S(2)}) copy-start(bf16[12,64,128]{2,1,0:T(8,128)(2,1)} %param.10) | copy-start | bytes 589828
  7.4 49.6 %copy-start.1 = (bf16[12,8,128]{2,1,0:T(8,128)(2,1)S(1)}, bf16[12,8,128]{2,1,0:T(8,128)(2,1)}, u32[]{:S(2)}) copy-start(bf16[12,8,128]{2,1,0:T(8,128)(2,1)} %param.11) | copy-start | bytes 73732
  9.1 22.0 %all-to-all-start = ((s32[8,1,12]{2,1,0:T(1,128)}), s32[8,1,12]{2,1,0:T(1,128)S(1)}, u32[]{:S(2)}, u32[]{:S(2)}) async-start(s32[8,1,12]{2,1,0:T(1,128)} %bitcast.13), calls=%async_computation | async-start | bytes 8192 | tf_op jit(solution)/shard_map/all_to_all | solution.py:60
  16.3 224.1 %all-gather.2.cloned.1.call-start = ((), (), s32[]{:S(2)}) async-start(), calls=%async_computation.5 | async-start | bytes 1081344 | tf_op jit(solution)/shard_map/all_gather | solution.py:106
  16.4 14.9 %collective-permute-start = (bf16[1,1,8,256]{3,2,1,0:T(8,128)(2,1)}, bf16[1,1,8,256]{3,2,1,0:T(8,128)(2,1)S(1)}, u32[]{:S(2)}, u32[]{:S(2)}) collective-permute-start(bf16[1,1,8,256]{3,2,1,0:T(8,128)(2,1)} %bitcast.136), channel_id=1, source_target_pairs={{0,1},{1,0},{2,3},{3,2},{4,5},{5,4},{6,7},{7,6},{8,9},{9,8},{10,11... | collective-permute-start | bytes 12296 | tf_op jit(solution)/shard_map/ppermute | solution.py:21
  32.0 3.7 %collective-permute-start.1 = (bf16[2,1,8,256]{3,2,0,1:T(8,128)(2,1)S(1)}, bf16[2,1,8,256]{3,2,0,1:T(8,128)(2,1)S(1)}, u32[]{:S(2)}, u32[]{:S(2)}) collective-permute-start(bf16[2,1,8,256]{3,2,0,1:T(8,128)(2,1)S(1)} %get-tuple-element.115), channel_id=1, source_target_pairs={{0,2},{1,3},{2,0},{3,1},{4,6},{5,7},{6,4},{7,5},{8,10},{9,11},{10,... | collective-permute-start | bytes 24584 | tf_op jit(solution)/shard_map/ppermute | solution.py:21
  35.7 8.0 %collective-permute-start.2 = (bf16[4,1,8,256]{3,2,0,1:T(8,128)(2,1)S(1)}, bf16[4,1,8,256]{3,2,0,1:T(8,128)(2,1)S(1)}, u32[]{:S(2)}, u32[]{:S(2)}) collective-permute-start(bf16[4,1,8,256]{3,2,0,1:T(8,128)(2,1)S(1)} %bitcast.127), channel_id=1, source_target_pairs={{0,4},{1,5},{2,6},{3,7},{4,0},{5,1},{6,2},{7,3},{8,12},{9,13},{10,... | collective-permute-start | bytes 49160 | tf_op jit(solution)/shard_map/ppermute | solution.py:21
  39.2 11.4 %all-to-all-start.1 = ((bf16[8,3,8,128]{3,2,1,0:T(8,128)(2,1)}), bf16[8,3,8,128]{3,2,1,0:T(8,128)(2,1)S(1)}, u32[]{:S(2)}, u32[]{:S(2)}) async-start(bf16[8,3,8,128]{3,2,1,0:T(8,128)(2,1)} %copy.31), calls=%async_computation.1 | async-start | bytes 98304 | tf_op jit(solution)/shard_map/all_to_all | solution.py:74
  43.7 10.3 %collective-permute-start.3 = (bf16[8,1,8,256]{3,2,0,1:T(8,128)(2,1)S(1)}, bf16[8,1,8,256]{3,2,0,1:T(8,128)(2,1)S(1)}, u32[]{:S(2)}, u32[]{:S(2)}) collective-permute-start(bf16[8,1,8,256]{3,2,0,1:T(8,128)(2,1)S(1)} %bitcast.125), channel_id=1, source_target_pairs={{0,8},{1,9},{2,10},{3,11},{4,12},{5,13},{6,14},{7,15},{8,0},{9,1},... | collective-permute-start | bytes 98312 | tf_op jit(solution)/shard_map/ppermute | solution.py:21
  50.5 16.3 %all-to-all-start.2 = ((bf16[8,3,64,128]{3,2,1,0:T(8,128)(2,1)}), bf16[8,3,64,128]{3,2,1,0:T(8,128)(2,1)S(1)}, u32[]{:S(2)}, u32[]{:S(2)}) async-start(bf16[8,3,64,128]{3,2,1,0:T(8,128)(2,1)} %copy.33), calls=%async_computation.2 | async-start | bytes 786432 | tf_op jit(solution)/shard_map/all_to_all | solution.py:73
  54.0 270.4 %reduce-scatter.2.cloned.1.call-start = ((), (), s32[]{:S(2)}) async-start(), calls=%async_computation.4 | async-start | bytes 245760 | tf_op jit(solution)/shard_map/reduce_scatter | solution.py:100
  54.1 12.7 %collective-permute-start.4 = (bf16[16,1,8,256]{3,2,0,1:T(8,128)(2,1)S(1)}, bf16[16,1,8,256]{3,2,0,1:T(8,128)(2,1)S(1)}, u32[]{:S(2)}, u32[]{:S(2)}) collective-permute-start(bf16[16,1,8,256]{3,2,0,1:T(8,128)(2,1)S(1)} %bitcast.122), channel_id=1, source_target_pairs={{0,16},{1,17},{2,18},{3,19},{4,20},{5,21},{6,22},{7,23},{8,24},{9,... | collective-permute-start | bytes 196616 | tf_op jit(solution)/shard_map/ppermute | solution.py:21
Sparse Core Ops, SparseCore 0:
  20.8 57.6 all-gather.1
Sparse Core Ops, SparseCore 1:
  240.5 19.1 reduce-scatter.1
